TPU v7x, 1024 devices: a whole 4x4x32 slice. The times are simulated.
1024 devices in a mesh: ctx: 256 (over x_hi, z, y), panel: 4 (over x_lo, core).
Axes of the slice: x: 4 (x_hi: 2, x_lo: 2; x = x_hi * 2 + x_lo), y: 4, z: 32, core: 2. Of those that a mesh axis runs over, the one named last changes fastest.
Arguments:
- se_streams: bfloat16 [3, 36864, 4096], P(None, 'ctx', 'panel'), may hold values from -6 to 6
- se_short: float32 [3, 3, 4096], P(None, None, 'panel'), may hold values from -2 to 2
- se_filter: float32 [7, 4096], P(None, 'panel'), may hold values from -2 to 2
- medium_projected_streams: bfloat16 [3, 36864, 4096], P(None, 'ctx', 'panel'), may hold values from -6 to 6
- mr_short: float32 [3, 3, 4096], P(None, None, 'panel'), may hold values from -2 to 2
- medium_filter_raw: float32 [128, 4096], P(None, 'panel'), may hold values from -0.9 to 0.9
- mr_decay: float32 [4096], P('panel'), may hold values from 0.003 to 0.1
- queries: bfloat16 [36864, 4096], P('ctx', 'panel'), may hold values from -180 to 180
- keys: bfloat16 [36864, 4096], P('ctx', 'panel'), may hold values from -6 to 6
- values: bfloat16 [36864, 4096], P('ctx', 'panel'), may hold values from -6 to 6
Outputs:
- se_out: bfloat16 [36864, 4096], P('ctx', 'panel')
- mr_out: bfloat16 [36864, 4096], P('ctx', 'panel')
- attn_out: bfloat16 [36864, 4096], P('ctx', 'panel')
All inputs are finite; a program needn't handle non-finite values.
Results may differ from a plain program's by a relative error of at most 0.008.
Values may be sent and summed in bfloat16 or wider, within the bound.
A program may use at most 32 MiB of HBM per device.

v0:
```python
import math

import jax
import jax.numpy as jnp
from jax import lax
from jax.sharding import PartitionSpec as P

CHANNEL_SHARD = 4096
HD = 128
FEATURIZER_TAPS = 3
LSE = 7
MEDIUM_TAPS = 128


def from_behind(value, axis, steps):
    count = lax.axis_size(axis)
    first, last = (max(0, -steps), min(count, count - steps))
    return lax.ppermute(value, axis, [(source, source + steps) for source in range(first, last)])


def featurize(ext, short):
    taps = short.shape[1]
    count = ext.shape[1]
    total = short[:, 0][:, None, :] * ext[:, taps - 1 : count, :].astype(jnp.float32)
    for j in range(1, taps):
        total = total + short[:, j][:, None, :] * ext[:, taps - 1 - j : count - j, :].astype(
            jnp.float32
        )
    return total


def long_conv(product, filt):
    channels = filt.shape[1]
    reversed_taps = filt[::-1][:, None, :]
    signal = product.astype(jnp.float32)[None]
    result = lax.conv_general_dilated(
        signal,
        reversed_taps,
        (1,),
        "VALID",
        dimension_numbers=("NWC", "WIO", "NWC"),
        feature_group_count=channels,
        precision=lax.Precision.HIGHEST,
    )
    return result[0]


def attend(qblk, kblk, value_block, qpos, kpos):
    heads = qblk.shape[1] // HD
    q3 = qblk.reshape(-1, heads, HD)
    k3 = kblk.reshape(-1, heads, HD)
    v3 = value_block.reshape(-1, heads, HD)
    scores = jnp.einsum("qhd,khd->hqk", q3, k3, preferred_element_type=jnp.float32) * (
        1.0 / math.sqrt(HD)
    )
    valid = (kpos[None, :] >= 0) & (kpos[None, :] <= qpos[:, None])
    masked = jnp.where(valid[None], scores, -1e30)
    top = jnp.max(masked, axis=-1, keepdims=True)
    raw = jnp.exp(masked - top)
    total = jnp.sum(raw, axis=-1)
    probs = raw.astype(jnp.bfloat16)
    out = jnp.einsum("hqk,khd->qhd", probs, v3, preferred_element_type=jnp.float32)
    out = out / total.T[:, :, None]
    return out.reshape(qblk.shape[0], -1)


def body(
    se_streams,
    se_short,
    se_filter,
    medium_projected_streams,
    mr_short,
    medium_filter_raw,
    mr_decay,
    queries,
    keys,
    values,
):
    token_rows = se_streams.shape[1]
    step_index = jnp.arange(MEDIUM_TAPS, dtype=jnp.float32)
    mr_taps = medium_filter_raw * jnp.exp(-mr_decay[None, :] * step_index[:, None])
    se_rim, mr_rim = from_behind(
        (
            se_streams[:, token_rows - (FEATURIZER_TAPS + LSE - 2) :, :],
            medium_projected_streams[:, token_rows - (FEATURIZER_TAPS + MEDIUM_TAPS - 2) :, :],
        ),
        "ctx",
        1,
    )
    se_feats = featurize(jnp.concatenate([se_rim, se_streams], axis=1), se_short)
    mr_feats = featurize(jnp.concatenate([mr_rim, medium_projected_streams], axis=1), mr_short)
    se_prod = (se_feats[1] * se_feats[2]).astype(jnp.bfloat16)
    mr_prod = (mr_feats[1] * mr_feats[2]).astype(jnp.bfloat16)
    se_mix = se_feats[0][-token_rows:] * long_conv(se_prod, se_filter)
    mr_mix = mr_feats[0][-token_rows:] * long_conv(mr_prod, mr_taps)
    key_prev, value_prev = from_behind((keys, values), "ctx", 1)
    start_offset = lax.axis_index("ctx") * token_rows
    local = jnp.arange(token_rows, dtype=jnp.int32)
    wide = jnp.arange(2 * token_rows, dtype=jnp.int32)
    attn_mix = attend(
        queries,
        jnp.concatenate([key_prev, keys], axis=0),
        jnp.concatenate([value_prev, values], axis=0),
        start_offset + local,
        start_offset - token_rows + wide,
    )
    sums = lax.psum(
        (
            jnp.sum(se_mix * se_mix, axis=-1),
            jnp.sum(mr_mix * mr_mix, axis=-1),
            jnp.sum(attn_mix * attn_mix, axis=-1),
        ),
        "panel",
    )
    outputs = []
    for mixed, square in zip((se_mix, mr_mix, attn_mix), sums):
        scale = lax.rsqrt(square / CHANNEL_SHARD + 1e-06)
        outputs.append((mixed * scale[:, None]).astype(jnp.bfloat16))
    return (outputs[0], outputs[1], outputs[2])


def solution(mesh):
    placed = (
        P(None, "ctx", "panel"),
        P(None, None, "panel"),
        P(None, "panel"),
        P(None, "ctx", "panel"),
        P(None, None, "panel"),
        P(None, "panel"),
        P("panel"),
        P("ctx", "panel"),
        P("ctx", "panel"),
        P("ctx", "panel"),
    )
    return jax.shard_map(
        body,
        mesh=mesh,
        in_specs=placed,
        out_specs=(P("ctx", "panel"), P("ctx", "panel"), P("ctx", "panel")),
        check_vma=False,
    )
```

profile of v0, /device:TPU:7, one launch (start us, length us, event | category | flops | bytes accessed | tf_op | source)
XLA Modules:
  0.0 83.3 jit_solution(8219812874160600455)
XLA Ops:
  0.7 0.9 %slice.67 = bf16[3,8,1024]{2,1,0:T(8,128)(2,1)S(1)} slice(bf16[3,144,1024]{2,1,0:T(8,128)(2,1)} %param.10), slice={[0:3], [136:144], [0:1024]} | slice | bytes 98304 | tf_op jit(solution)/shard_map/slice | solution.py:84
  1.6 3.3 %collective-permute-start = (bf16[3,8,1024]{2,1,0:T(8,128)(2,1)S(1)}, bf16[3,8,1024]{2,1,0:T(8,128)(2,1)S(1)}, u32[]{:S(2)}, u32[]{:S(2)}) collective-permute-start(bf16[3,8,1024]{2,1,0:T(8,128)(2,1)S(1)} %slice.67), channel_id=1, source_target_pairs={{0,4},{4,8},{8,12},{12,16},{16,20},{20,24},{24,28},{28,32},{32,36}... | collective-permute-start | bytes 147464 | tf_op jit(solution)/shard_map/ppermute | solution.py:18
  4.9 2.3 %slice.77 = bf16[3,129,1024]{2,1,0:T(8,128)(2,1)} slice(bf16[3,144,1024]{2,1,0:T(8,128)(2,1)} %param.13), slice={[0:3], [15:144], [0:1024]} | slice | bytes 1585152 | tf_op jit(solution)/shard_map/slice | solution.py:85
  7.2 3.2 %collective-permute-start.1 = (bf16[3,129,1024]{2,1,0:T(8,128)(2,1)}, bf16[3,129,1024]{2,1,0:T(8,128)(2,1)}, u32[]{:S(2)}, u32[]{:S(2)}) collective-permute-start(bf16[3,129,1024]{2,1,0:T(8,128)(2,1)} %slice.77), channel_id=1, source_target_pairs={{0,4},{4,8},{8,12},{12,16},{16,20},{20,24},{24,28},{28,32},{32,36}... | collective-permute-start | bytes 2377736 | tf_op jit(solution)/shard_map/ppermute | solution.py:18
  10.4 2.9 %collective-permute-start.3 = (bf16[144,1024]{1,0:T(8,128)(2,1)}, bf16[144,1024]{1,0:T(8,128)(2,1)}, u32[]{:S(2)}, u32[]{:S(2)}) collective-permute-start(bf16[144,1024]{1,0:T(8,128)(2,1)} %param.18), channel_id=1, source_target_pairs={{0,4},{4,8},{8,12},{12,16},{16,20},{20,24},{24,28},{28,32},{32,36}... | collective-permute-start | bytes 884744 | tf_op jit(solution)/shard_map/ppermute | solution.py:18
  13.3 3.2 %collective-permute-start.2 = (bf16[144,1024]{1,0:T(8,128)(2,1)}, bf16[144,1024]{1,0:T(8,128)(2,1)}, u32[]{:S(2)}, u32[]{:S(2)}) collective-permute-start(bf16[144,1024]{1,0:T(8,128)(2,1)} %param.19), channel_id=1, source_target_pairs={{0,4},{4,8},{8,12},{12,16},{16,20},{20,24},{24,28},{28,32},{32,36}... | collective-permute-start | bytes 884744 | tf_op jit(solution)/shard_map/ppermute | solution.py:18
  16.6 0.9 %fusion.38 = (f32[3,1,1024]{2,1,0:T(1,128)S(1)}, f32[3,1,1024]{2,1,0:T(1,128)S(1)}, f32[3,1,1024]{2,1,0:T(1,128)S(1)}) fusion(f32[3,3,1024]{2,1,0:T(4,128)} %param.11), kind=kLoop, calls=%fused_computation.68 | loop fusion | bytes 73728 | tf_op jit(solution)/shard_map/slice | solution.py:24
  18.1 2.7 %rev.7 = f32[128,1024]{1,0:T(8,128)} reverse(f32[128,1024]{1,0:T(8,128)S(1)} %exponential_multiply_fusion), dimensions={0} | reverse | bytes 1048576 | tf_op jit(solution)/shard_map/rev | solution.py:34
  20.8 4.1 %collective-permute-done = bf16[3,8,1024]{2,1,0:T(8,128)(2,1)S(1)} collective-permute-done((bf16[3,8,1024]{2,1,0:T(8,128)(2,1)S(1)}, bf16[3,8,1024]{2,1,0:T(8,128)(2,1)S(1)}, u32[]{:S(2)}, u32[]{:S(2)}) %collective-permute-start) | collective-permute-done | bytes 49184 | tf_op jit(solution)/shard_map/ppermute | solution.py:18
  26.6 1.2 %copy.32 = f32[8,19,1024]{2,1,0:T(8,128)} copy(f32[8,19,1024]{2,0,1:T(8,128)S(1)} %convolution_select_fusion) | data formatting | bytes 1245184 | tf_op jit(solution)/shard_map/conv_general_dilated | solution.py:36
  27.8 1.2 %reshape.93 = f32[1,152,1024]{2,1,0:T(8,128)S(1)} reshape(f32[8,19,1024]{2,1,0:T(8,128)} %copy.32) | data formatting | bytes 1245184 | tf_op jit(solution)/shard_map/conv_general_dilated | solution.py:36
  29.2 23.3 %collective-permute-done.3 = bf16[144,1024]{1,0:T(8,128)(2,1)} collective-permute-done((bf16[144,1024]{1,0:T(8,128)(2,1)}, bf16[144,1024]{1,0:T(8,128)(2,1)}, u32[]{:S(2)}, u32[]{:S(2)}) %collective-permute-start.3) | collective-permute-done | bytes 294944 | tf_op jit(solution)/shard_map/ppermute | solution.py:18
  52.5 1.6 %fusion.39 = (f32[8,144]{1,0:T(8,128)S(1)}, f32[8,144,288]{2,1,0:T(8,128)S(1)}) fusion(pred[144,288]{1,0:T(8,128)(4,1)S(1)} %compare_and_fusion, bf16[144,1024]{1,0:T(8,128)(2,1)S(1)} %copy-done.9, bf16[144,1024]{1,0:T(8,128)(2,1)} %collective-permute-done.3, bf16[144,1024]{1,0:T(8,128)(2,1)S(1)} %copy-done), kind=kOutput, calls=%fused_computation.69 | convolution fusion | flops 87108480 | bytes 2257920 | tf_op jit(solution)/shard_map/qhd,khd->hqk/dot_general | solution.py:53
  54.1 0.8 %fusion = f32[8,144]{1,0:T(8,128)S(1)} fusion(f32[8,144,288]{2,1,0:T(8,128)S(1)} %get-tuple-element.13, f32[8,144]{1,0:T(8,128)S(1)} %get-tuple-element.12), kind=kLoop, calls=%fused_computation.4 | loop fusion | flops 662400 | bytes 1336320 | tf_op jit(solution)/shard_map/reduce_sum | solution.py:60
  54.9 3.9 %collective-permute-done.2 = bf16[144,1024]{1,0:T(8,128)(2,1)} collective-permute-done((bf16[144,1024]{1,0:T(8,128)(2,1)}, bf16[144,1024]{1,0:T(8,128)(2,1)}, u32[]{:S(2)}, u32[]{:S(2)}) %collective-permute-start.2) | collective-permute-done | bytes 294944 | tf_op jit(solution)/shard_map/ppermute | solution.py:18
  58.8 2.5 %multiply_reduce_fusion = (f32[144]{0:T(256)S(1)}, f32[144,8,128]{2,0,1:T(8,128)}) fusion(f32[144,8]{0,1:T(8,128)S(1)} %bitcast.77, f32[8,144,288]{2,1,0:T(8,128)S(1)} %get-tuple-element.13, f32[8,144]{1,0:T(8,128)S(1)} %get-tuple-element.12, bf16[144,1024]{1,0:T(8,128)(2,1)S(1)} %copy-done.10, bf16[144,1024]{1,0:T(8,128)(2,1)} %collective-permute-done.2), kind=kOutput, calls=%fused_computation.35 | convolution fusion | flops 87220080 | bytes 2516544 | tf_op jit(solution)/shard_map/hqk,khd->qhd/dot_general | solution.py:62
  61.3 1.9 %copy_dynamic-update-slice_fusion.1 = bf16[3,273,1024]{2,0,1:T(4,128)(2,1)S(1)} fusion(bf16[3,129,1024]{2,1,0:T(8,128)(2,1)} %collective-permute-done.1), kind=kLoop, calls=%fused_computation.14 | loop fusion | bytes 1849344
  63.2 0.8 %copy_dynamic-update-slice_fusion = bf16[3,273,1024]{2,0,1:T(4,128)(2,1)S(1)} fusion(bf16[3,273,1024]{2,0,1:T(4,128)(2,1)S(1)} %copy_dynamic-update-slice_fusion.1, bf16[3,144,1024]{2,1,0:T(8,128)(2,1)S(1)} %copy-done.1), kind=kLoop, calls=%fused_computation.9 | loop fusion | bytes 2064384 | tf_op jit(solution)/shard_map/concatenate | solution.py:91
  64.1 2.9 %multiply_add_fusion = f32[3,271,1024]{2,0,1:T(4,128)S(1)} fusion(bf16[3,273,1024]{2,0,1:T(4,128)(2,1)S(1)} %copy_dynamic-update-slice_fusion, f32[3,1024]{1,0:T(4,128)S(1)} %get-tuple-element.18, f32[3,1024]{1,0:T(4,128)S(1)} %get-tuple-element.19, f32[3,1024]{1,0:T(4,128)S(1)} %bitcast.74), kind=kLoop, calls=%fused_computation | loop fusion | flops 6660096 | bytes 8361984 | tf_op jit(solution)/shard_map/add | solution.py:26
  67.0 7.3 %slice_multiply_fusion.2 = f32[1,144,1024]{2,0,1:T(1,128)S(1)} fusion(f32[3,271,1024]{2,0,1:T(4,128)S(1)} %multiply_add_fusion, f32[128,1,1024]{2,0,1:T(8,128)S(1)} %bitcast.73), kind=kOutput, calls=%fused_computation.26 | convolution fusion | flops 227194880 | bytes 3923968 | tf_op jit(solution)/shard_map/conv_general_dilated | solution.py:36
  74.5 6.3 %all-reduce = (f32[144]{0:T(256)S(1)}, f32[144]{0:T(256)S(1)}, f32[144]{0:T(256)S(1)}) all-reduce(f32[144]{0:T(256)S(1)} %multiply_reduce_fusion.1, f32[144]{0:T(256)S(1)} %fusion.17, f32[144]{0:T(256)S(1)} %get-tuple-element.14), channel_id=1, replica_groups=mesh['ctx'=256,'panel'=4] {'panel'}, use_global_device_ids=true, to_apply=%region_1.2 | all-reduce | flops 432 | bytes 3456 | tf_op jit(solution)/shard_map/psum | solution.py:107
  80.7 0.8 multiply_convert_fusion
  81.6 0.9 %fusion.18 = bf16[144,1024]{1,0:T(8,128)(2,1)} fusion(f32[1,144,1024]{2,0,1:T(1,128)S(1)} %slice_multiply_fusion.2, f32[144]{0:T(256)S(1)} %add_rsqrt_fusion.1), kind=kLoop, calls=%fused_computation.34 | loop fusion | flops 294912 | bytes 885312 | tf_op jit(solution)/shard_map/convert_element_type | solution.py:118
  82.5 0.8 fusion.11
  (51 shorter events, 2.6 us)
Async XLA Ops:
  0.6 51.9 %copy-start = (bf16[144,1024]{1,0:T(8,128)(2,1)S(1)}, bf16[144,1024]{1,0:T(8,128)(2,1)}, u32[]{:S(2)}) copy-start(bf16[144,1024]{1,0:T(8,128)(2,1)} %param.17) | copy-start | bytes 884740
  0.6 16.9 %copy-start.7 = (f32[3,3,1024]{2,1,0:T(4,128)S(1)}, f32[3,3,1024]{2,1,0:T(4,128)}, u32[]{:S(2)}) copy-start(f32[3,3,1024]{2,1,0:T(4,128)} %param.14) | copy-start | bytes 110596
  0.7 16.9 %copy-start.8 = (f32[1024]{0:T(1024)S(1)}, f32[1024]{0:T(1024)}, u32[]{:S(2)}) copy-start(f32[1024]{0:T(1024)} %param.16) | copy-start | bytes 12292
  0.7 16.9 %copy-start.4 = (f32[128,1024]{1,0:T(8,128)S(1)}, f32[128,1024]{1,0:T(8,128)}, u32[]{:S(2)}) copy-start(f32[128,1024]{1,0:T(8,128)} %param.15) | copy-start | bytes 1572868
  0.7 17.2 %copy-start.6 = (f32[7,1024]{1,0:T(8,128)S(1)}, f32[7,1024]{1,0:T(8,128)}, u32[]{:S(2)}) copy-start(f32[7,1024]{1,0:T(8,128)} %param.12) | copy-start | bytes 86020
  1.6 23.3 %copy-start.2 = (bf16[3,144,1024]{2,1,0:T(8,128)(2,1)S(1)}, bf16[3,144,1024]{2,1,0:T(8,128)(2,1)}, u32[]{:S(2)}) copy-start(bf16[3,144,1024]{2,1,0:T(8,128)(2,1)} %param.10) | copy-start | bytes 2654212
  1.6 23.3 %collective-permute-start = (bf16[3,8,1024]{2,1,0:T(8,128)(2,1)S(1)}, bf16[3,8,1024]{2,1,0:T(8,128)(2,1)S(1)}, u32[]{:S(2)}, u32[]{:S(2)}) collective-permute-start(bf16[3,8,1024]{2,1,0:T(8,128)(2,1)S(1)} %slice.67), channel_id=1, source_target_pairs={{0,4},{4,8},{8,12},{12,16},{16,20},{20,24},{24,28},{28,32},{32,36}... | collective-permute-start | bytes 147464 | tf_op jit(solution)/shard_map/ppermute | solution.py:18
  7.2 54.1 %collective-permute-start.1 = (bf16[3,129,1024]{2,1,0:T(8,128)(2,1)}, bf16[3,129,1024]{2,1,0:T(8,128)(2,1)}, u32[]{:S(2)}, u32[]{:S(2)}) collective-permute-start(bf16[3,129,1024]{2,1,0:T(8,128)(2,1)} %slice.77), channel_id=1, source_target_pairs={{0,4},{4,8},{8,12},{12,16},{16,20},{20,24},{24,28},{28,32},{32,36}... | collective-permute-start | bytes 2377736 | tf_op jit(solution)/shard_map/ppermute | solution.py:18
  10.4 42.1 %collective-permute-start.3 = (bf16[144,1024]{1,0:T(8,128)(2,1)}, bf16[144,1024]{1,0:T(8,128)(2,1)}, u32[]{:S(2)}, u32[]{:S(2)}) collective-permute-start(bf16[144,1024]{1,0:T(8,128)(2,1)} %param.18), channel_id=1, source_target_pairs={{0,4},{4,8},{8,12},{12,16},{16,20},{20,24},{24,28},{28,32},{32,36}... | collective-permute-start | bytes 884744 | tf_op jit(solution)/shard_map/ppermute | solution.py:18
  13.3 45.5 %collective-permute-start.2 = (bf16[144,1024]{1,0:T(8,128)(2,1)}, bf16[144,1024]{1,0:T(8,128)(2,1)}, u32[]{:S(2)}, u32[]{:S(2)}) collective-permute-start(bf16[144,1024]{1,0:T(8,128)(2,1)} %param.19), channel_id=1, source_target_pairs={{0,4},{4,8},{8,12},{12,16},{16,20},{20,24},{24,28},{28,32},{32,36}... | collective-permute-start | bytes 884744 | tf_op jit(solution)/shard_map/ppermute | solution.py:18
  25.5 0.7 copy-start.11
  26.6 25.9 %copy-start.9 = (bf16[144,1024]{1,0:T(8,128)(2,1)S(1)}, bf16[144,1024]{1,0:T(8,128)(2,1)}, u32[]{:S(2)}) copy-start(bf16[144,1024]{1,0:T(8,128)(2,1)} %param.18) | copy-start | bytes 884740
  29.2 29.6 %copy-start.10 = (bf16[144,1024]{1,0:T(8,128)(2,1)S(1)}, bf16[144,1024]{1,0:T(8,128)(2,1)}, u32[]{:S(2)}) copy-start(bf16[144,1024]{1,0:T(8,128)(2,1)} %param.19) | copy-start | bytes 884740
  61.3 1.9 %copy-start.1 = (bf16[3,144,1024]{2,1,0:T(8,128)(2,1)S(1)}, bf16[3,144,1024]{2,1,0:T(8,128)(2,1)}, u32[]{:S(2)}) copy-start(bf16[3,144,1024]{2,1,0:T(8,128)(2,1)} %param.13) | copy-start | bytes 2654212
  64.1 2.9 %copy-start.5 = (f32[128,1024]{1,0:T(8,128)S(1)}, f32[128,1024]{1,0:T(8,128)}, u32[]{:S(2)}) copy-start(f32[128,1024]{1,0:T(8,128)} %rev.7) | copy-start | bytes 1572868
  80.7 1.7 %copy-start.3 = (f32[144,8,128]{2,0,1:T(8,128)S(1)}, f32[144,8,128]{2,0,1:T(8,128)}, u32[]{:S(2)}) copy-start(f32[144,8,128]{2,0,1:T(8,128)} %get-tuple-element.15) | copy-start | bytes 1769476
where the time goes:
time: 83.9 us; the launch traced here: 83.3 us
  waiting for transfers between devices  31.3 us (37%)
  local copies, waits for them, and re-layouts  12.9 us (15%)
  starting transfers between devices  12.6 us (15%)
  matrix products  11.7 us (14%)
  other arithmetic  7.55 us (9%)
  blocking collectives  6.27 us (7%)
  between operations  0.97 us (1%)
    ppermute x4, waiting for transfers between devices, from_behind(): lax.ppermute(value, axis, [(source, source + steps) for source in range(f...  31.3 us
    ppermute x4, starting transfers between devices, from_behind(): lax.ppermute(value, axis, [(source, source + steps) for source in range(f...  12.6 us
    conv_general_dilated x2, matrix products, long_conv(): lax.conv_general_dilated(signal, reversed_taps, (1,), 'VALID', dimension_...  7.63 us
    psum x1, blocking collectives, body(): lax.psum((jnp.sum(se_mix * se_mix, axis=-1), jnp.sum(mr_mix * mr_mix, axi...  6.27 us
    add x2, other arithmetic, featurize(): total + short[:, j][:, None, :] * ext[:, taps - 1 - j:count - j, :].astyp...  3.53 us
    rev x2, local copies, waits for them, and re-layouts, long_conv(): reversed_taps = filt[::-1][:, None, :]  2.89 us
    conv_general_dilated x5, local copies, waits for them, and re-layouts, long_conv(): lax.conv_general_dilated(signal, reversed_taps, (1,), 'VALID', dimension_...  2.78 us
    convert_element_type x3, other arithmetic, body(): outputs.append((mixed * scale[:, None]).astype(jnp.bfloat16))  2.53 us
  transfers between devices with their start and end apart: 4, of which 3 were waited for; matrix products, arithmetic and copies ran while one was open for 18% of the time, Pallas kernels for 0%

commit v1 on v0

v1 whole, which is shorter than its diff:
```python
import functools
import math

import jax
import jax.numpy as jnp
from jax import lax
from jax.experimental import pallas as pl
from jax.experimental.pallas import tpu as pltpu
from jax.sharding import PartitionSpec as P

CHANNELS = 4096
HD = 128
T = 144
TAPS = 128
LSE = 7
HEADS = 8
WIDTH = HEADS * HD
F32 = jnp.float32
BF16 = jnp.bfloat16
MESH = pl.DeviceIdType.MESH
HIGHEST = lax.Precision.HIGHEST


def rows(t, count):
    return pl.ds(pl.multiple_of(t * 8, 8), count * 8)


def to_time(src, dst, start):
    def step(i, carry):
        r = pl.multiple_of(i * 16, 16)
        x = src[pl.ds(r, 16), :].astype(F32)
        for half in range(2):
            for k in range(8):
                dst[pl.ds((start + r + half * 8) * 8 + k, 8, stride=8), :] = x[
                    half * 8 : half * 8 + 8, k * HD : (k + 1) * HD
                ]
        return carry

    lax.fori_loop(0, T // 16, step, 0)


def spread(value, count):
    return jnp.concatenate([value] * count, axis=0)


def feature(u, w, base, t, count):
    total = spread(w[rows(base, 1), :], count) * u[rows(t + 2, count), :]
    for j in range(1, 3):
        total = total + spread(w[rows(base + j, 1), :], count) * u[rows(t + 2 - j, count), :]
    return total


def kernel(
    n_ctx, n_panel,
    se_u, se_w, se_f, mr_u, mr_w, mr_raw, decay, q, k, v,
    se_out, mr_out, at_out,
    ub, wb, fb, rawb, decb, qb, kcat, vcat,
    ut, wt, ft, taps, se_p, mr_p, se_mix, mr_mix, at_mix, bias, sq,
    rim_out, rim_in, p_out, p_in, st_out, st_in,
    load_sem, rim_sem, p_sem, k_send, k_recv, v_send, v_recv,
    st_send, st_recv,
):
    c = lax.axis_index("ctx")
    p = lax.axis_index("panel")
    is_first = c == 0
    has_dst = c < n_ctx - 1
    dst = (lax.rem(c + 1, n_ctx), p)
    src = (lax.rem(c + n_ctx - 1, n_ctx), p)

    loads = []

    def load(source, target):
        copy = pltpu.make_async_copy(source, target, load_sem.at[len(loads)])
        copy.start()
        loads.append(copy)
        return copy

    l_mr = [load(mr_u.at[i], ub.at[3 + i]) for i in (1, 2)]
    l_mw = load(mr_w, wb.at[1])
    l_sw = load(se_w, wb.at[0])
    l_se = [load(se_u.at[i], ub.at[i]) for i in (1, 2)]
    l_m0 = load(mr_u.at[0], ub.at[3])
    l_s0 = load(se_u.at[0], ub.at[0])
    l_f = load(se_f, fb)
    l_raw = load(mr_raw, rawb)
    l_dec = load(decay, decb)
    l_q = load(q, qb)
    l_k = load(k, kcat.at[pl.ds(T, T), :])
    l_v = load(v, vcat.at[pl.ds(T, T), :])

    barrier = pltpu.get_barrier_semaphore()

    @pl.when(jnp.logical_not(is_first))
    def _():
        pl.semaphore_signal(barrier, inc=1, device_id=src, device_id_type=MESH)

    for r in range(1, n_panel):
        pl.semaphore_signal(
            barrier, inc=1, device_id=(c, lax.rem(p + r, n_panel)), device_id_type=MESH
        )

    l_mw.wait()
    l_sw.wait()
    for b in range(2):
        for i in range(3):
            for j in range(3):
                for kk in range(8):
                    wt[pl.ds((b * 9 + i * 3 + j) * 8 + kk, 1), :] = wb[
                        b, i, pl.ds(j, 1), kk * HD : (kk + 1) * HD
                    ]
    zero_halo = jnp.zeros((16, HD), F32)
    for i in range(6):
        ut[i, pl.ds(0, 16), :] = zero_halo

    def products(block, out, shift, t, count):
        first = feature(ut.at[block * 3 + 1], wt, block * 9 + 3, t, count)
        second = feature(ut.at[block * 3 + 2], wt, block * 9 + 6, t, count)
        rounded = (first * second).astype(BF16)
        out[rows(t + shift, count), :] = rounded.astype(F32)
        return rounded

    for copy in l_mr:
        copy.wait()
    for i in (4, 5):
        to_time(ub.at[i], ut.at[i], 2)

    def mr_low(i, carry):
        products(1, mr_p, TAPS, i * 8, 8)
        return carry

    def mr_high(i, carry):
        t = i * 8
        rounded = products(1, mr_p, TAPS, t, 8)
        p_out[rows(t - 16, 8), :] = rounded
        return carry

    lax.fori_loop(0, 2, mr_low, 0)
    lax.fori_loop(2, 18, mr_high, 0)

    for copy in l_se:
        copy.wait()
    for i in (1, 2):
        to_time(ub.at[i], ut.at[i], 2)

    def se_low(i, carry):
        products(0, se_p, 8, i * 8, 8)
        return carry

    lax.fori_loop(0, 17, se_low, 0)
    rim_out[pl.ds(0, 64), :] = products(0, se_p, 8, 136, 8)
    l_m0.wait()
    l_s0.wait()
    for i in (3, 0):
        to_time(ub.at[i], ut.at[i], 2)
    for i in range(6):
        rim_out[pl.ds(64 + i * 16, 16), :] = ut[i, pl.ds(T * 8, 16), :].astype(BF16)

    pl.semaphore_wait(barrier, (n_panel - 1) + has_dst.astype(jnp.int32))

    def head(h):
        return pl.ds(pl.multiple_of(h * HD, HD), HD)

    rim_copy = pltpu.make_async_remote_copy(
        rim_out, rim_in, rim_sem.at[0], rim_sem.at[1], device_id=dst, device_id_type=MESH
    )
    p_copy = pltpu.make_async_remote_copy(
        p_out, p_in, p_sem.at[0], p_sem.at[1], device_id=dst, device_id_type=MESH
    )

    def k_copy(h):
        return pltpu.make_async_remote_copy(
            k.at[:, head(h)], kcat.at[pl.ds(0, T), head(h)], k_send.at[h], k_recv.at[h],
            device_id=dst, device_id_type=MESH,
        )

    def v_copy(h):
        return pltpu.make_async_remote_copy(
            v.at[:, head(h)], vcat.at[pl.ds(0, T), head(h)], v_send.at[h], v_recv.at[h],
            device_id=dst, device_id_type=MESH,
        )

    @pl.when(has_dst)
    def _():
        rim_copy.start()
        p_copy.start()

        def send(h, carry):
            k_copy(h).start()
            v_copy(h).start()
            return carry

        lax.fori_loop(0, HEADS, send, 0)

    l_f.wait()
    for j in range(LSE):
        for kk in range(8):
            ft[pl.ds(j * 8 + kk, 1), :] = fb[pl.ds(j, 1), kk * HD : (kk + 1) * HD]
    l_raw.wait()
    l_dec.wait()

    def tap_rows(i, carry):
        r = pl.multiple_of(i * 8, 8)
        x = rawb[pl.ds(r, 8), :]
        for kk in range(8):
            taps[pl.ds(r * 8 + kk, 8, stride=8), :] = x[:, kk * HD : (kk + 1) * HD]
        return carry

    lax.fori_loop(0, TAPS // 8, tap_rows, 0)

    def tap_decay(j, carry):
        jf = j.astype(F32)
        taps[rows(j, 1), :] = taps[rows(j, 1), :] * jnp.exp(-decb[...] * jf)
        return carry

    lax.fori_loop(0, TAPS, tap_decay, 0)

    queries_at = lax.broadcasted_iota(jnp.int32, (T, 2 * T), 0)
    keys_at = lax.broadcasted_iota(jnp.int32, (T, 2 * T), 1)
    low = lax.select(is_first, T, 0)
    seen = jnp.logical_and(keys_at <= queries_at + T, keys_at >= low)
    bias[...] = jnp.where(seen, 0.0, -1e30)

    def when_fed(value):
        pl.when(jnp.logical_not(is_first))(value)

    @pl.when(is_first)
    def _():
        rim_in[...] = jnp.zeros((160, HD), BF16)
        p_in[...] = jnp.zeros((TAPS * 8, HD), BF16)
        kcat[pl.ds(0, T), :] = jnp.zeros((T, WIDTH), BF16)
        vcat[pl.ds(0, T), :] = jnp.zeros((T, WIDTH), BF16)

    when_fed(rim_copy.wait_recv)
    for i in range(6):
        ut[i, pl.ds(0, 16), :] = rim_in[pl.ds(64 + i * 16, 16), :].astype(F32)
    se_p[pl.ds(0, 64), :] = rim_in[pl.ds(0, 64), :].astype(F32)
    products(0, se_p, 8, 0, 2)
    products(1, mr_p, TAPS, 0, 2)

    def se_block(i, carry):
        t = i * 8
        total = spread(ft[pl.ds(0, 8), :], 8) * se_p[rows(t + 8, 8), :]
        for j in range(1, LSE):
            total = total + spread(ft[pl.ds(j * 8, 8), :], 8) * se_p[rows(t + 8 - j, 8), :]
        se_mix[rows(t, 8), :] = total * feature(ut.at[0], wt, 0, t, 8)
        return carry

    lax.fori_loop(0, T // 8, se_block, 0)

    when_fed(p_copy.wait_recv)

    def prev_p(i, carry):
        mr_p[rows(i * 8, 8), :] = p_in[rows(i * 8, 8), :].astype(F32)
        return carry

    lax.fori_loop(0, TAPS // 8, prev_p, 0)

    block = 16

    def mr_block(i, carry):
        t = i * block

        def tap_group(g, acc):
            j0 = g * 8
            acc = list(acc)
            window = [mr_p[rows(TAPS + t - j0 - 7 + s, 1), :] for s in range(block + 7)]
            for jj in range(8):
                tap = taps[rows(j0 + jj, 1), :]
                for s in range(block):
                    acc[s] = acc[s] + tap * window[s + 7 - jj]
            return tuple(acc)

        zero = jnp.zeros((8, HD), F32)
        acc = lax.fori_loop(0, TAPS // 8, tap_group, (zero,) * block)
        gate = feature(ut.at[3], wt, 9, t, block)
        for s in range(block):
            mr_mix[rows(t + s, 1), :] = acc[s] * gate[s * 8 : s * 8 + 8]
        return carry

    lax.fori_loop(0, T // block, mr_block, 0)

    def squares(mix, out_index):
        def step(i, carry):
            base = pl.multiple_of(i * 64, 64)
            total = jnp.zeros((8, HD), F32)
            for kk in range(8):
                x = mix[pl.ds(base + kk, 8, stride=8), :]
                total = total + x * x
            sq[out_index, pl.ds(pl.multiple_of(i * 8, 8), 8), :] = total
            return carry

        lax.fori_loop(0, T // 8, step, 0)

    ones = jnp.ones((8, HD), F32)

    def row_sums(index):
        return lax.dot_general(
            ones, sq[index], (((1,), (1,)), ((), ())),
            precision=HIGHEST, preferred_element_type=F32,
        )

    def st_copy(s, r):
        return pltpu.make_async_remote_copy(
            st_out.at[s], st_in.at[s, r - 1], st_send.at[s, r - 1], st_recv.at[s, r - 1],
            device_id=(c, lax.rem(p + r, n_panel)), device_id_type=MESH,
        )

    def share(s):
        for r in range(1, n_panel):
            st_copy(s, r).start()

    pick = (lax.broadcasted_iota(jnp.int32, (8, HD), 0) == 0).astype(F32)

    def scales(s, index):
        total = st_out[s, index, :, :T]
        for r in range(1, n_panel):
            total = total + st_in[s, r - 1, index, :, :T]
        scale = lax.rsqrt(total / CHANNELS + 1e-06)
        return lax.dot_general(
            scale, pick, (((0,), (0,)), ((), ())),
            precision=HIGHEST, preferred_element_type=F32,
        )

    squares(se_mix, 0)
    squares(mr_mix, 1)
    st_out[0, 0, :, :T] = row_sums(0)
    st_out[0, 1, :, :T] = row_sums(1)
    share(0)

    l_q.wait()
    l_k.wait()
    l_v.wait()
    sq[2] = jnp.zeros((T, HD), F32)

    def attend(h, carry):
        when_fed(k_copy(h).wait_recv)
        scores = lax.dot_general(
            qb[:, head(h)], kcat[:, head(h)], (((1,), (1,)), ((), ())),
            preferred_element_type=F32,
        )
        scores = scores * (1.0 / math.sqrt(HD)) + bias[...]
        top = jnp.max(scores, axis=1, keepdims=True)
        raw = jnp.exp(scores - top)
        total = jnp.sum(raw, axis=1, keepdims=True)
        when_fed(v_copy(h).wait_recv)
        mixed = lax.dot_general(
            raw.astype(BF16), vcat[:, head(h)], (((1,), (0,)), ((), ())),
            preferred_element_type=F32,
        )
        mixed = mixed * (1.0 / total)
        at_mix[:, head(h)] = mixed
        sq[2] = sq[2] + mixed * mixed
        return carry

    lax.fori_loop(0, HEADS - 2, attend, 0)

    for r in range(1, n_panel):
        st_copy(0, r).wait_recv()
    for index, mix, out in ((0, se_mix, se_out), (1, mr_mix, mr_out)):
        sq[index] = scales(0, index)

        def finish(i, carry):
            r = pl.multiple_of(i * 16, 16)
            for kk in range(8):
                parts = []
                for hh in range(2):
                    x = mix[pl.ds((r + hh * 8) * 8 + kk, 8, stride=8), :]
                    parts.append(x * sq[index, pl.ds(r + hh * 8, 8), :])
                out[pl.ds(r, 16), kk * HD : (kk + 1) * HD] = jnp.concatenate(parts, 0).astype(BF16)
            return carry

        lax.fori_loop(0, T // 16, finish, 0)

    lax.fori_loop(HEADS - 2, HEADS, attend, 0)

    st_out[1, 0, :, :T] = row_sums(2)
    share(1)
    for r in range(1, n_panel):
        st_copy(1, r).wait_recv()
    sq[2] = scales(1, 0)
    for h in range(HEADS):
        at_out[:, h * HD : (h + 1) * HD] = (at_mix[:, h * HD : (h + 1) * HD] * sq[2]).astype(BF16)

    for s in range(2):
        for r in range(1, n_panel):
            st_copy(s, r).wait_send()

    @pl.when(has_dst)
    def _():
        rim_copy.wait_send()
        p_copy.wait_send()

        def sent(h, carry):
            k_copy(h).wait_send()
            v_copy(h).wait_send()
            return carry

        lax.fori_loop(0, HEADS, sent, 0)


def body(n_ctx, n_panel, se_u, se_w, se_f, mr_u, mr_w, mr_raw, mr_decay, q, k, v):
    anywhere = pl.BlockSpec(memory_space=pl.ANY)
    vmem = pl.BlockSpec(memory_space=pltpu.VMEM)
    out = jax.ShapeDtypeStruct((T, WIDTH), BF16)
    dma = pltpu.SemaphoreType.DMA
    return pl.pallas_call(
        functools.partial(kernel, n_ctx, n_panel),
        out_shape=(out, out, out),
        in_specs=[anywhere] * 10,
        out_specs=(vmem, vmem, vmem),
        scratch_shapes=[
            pltpu.VMEM((6, T, WIDTH), BF16),
            pltpu.VMEM((2, 3, 3, WIDTH), F32),
            pltpu.VMEM((LSE, WIDTH), F32),
            pltpu.VMEM((TAPS, WIDTH), F32),
            pltpu.VMEM((8, HD), F32),
            pltpu.VMEM((T, WIDTH), BF16),
            pltpu.VMEM((2 * T, WIDTH), BF16),
            pltpu.VMEM((2 * T, WIDTH), BF16),
            pltpu.VMEM((6, (T + 2) * 8, HD), F32),
            pltpu.VMEM((18 * 8, HD), F32),
            pltpu.VMEM((8 * 8, HD), F32),
            pltpu.VMEM((TAPS * 8, HD), F32),
            pltpu.VMEM(((T + 8) * 8, HD), F32),
            pltpu.VMEM(((T + TAPS) * 8, HD), F32),
            pltpu.VMEM((T * 8, HD), F32),
            pltpu.VMEM((T * 8, HD), F32),
            pltpu.VMEM((T, WIDTH), F32),
            pltpu.VMEM((T, 2 * T), F32),
            pltpu.VMEM((3, T, HD), F32),
            pltpu.VMEM((160, HD), BF16),
            pltpu.VMEM((160, HD), BF16),
            pltpu.VMEM((TAPS * 8, HD), BF16),
            pltpu.VMEM((TAPS * 8, HD), BF16),
            pltpu.VMEM((2, 2, 8, 256), F32),
            pltpu.VMEM((2, n_panel - 1, 2, 8, 256), F32),
            dma((14,)),
            dma((2,)),
            dma((2,)),
            dma((HEADS,)),
            dma((HEADS,)),
            dma((HEADS,)),
            dma((HEADS,)),
            dma((2, n_panel - 1)),
            dma((2, n_panel - 1)),
        ],
        compiler_params=pltpu.CompilerParams(collective_id=0, has_side_effects=True),
        name="mixer",
    )(se_u, se_w, se_f, mr_u, mr_w, mr_raw, mr_decay.reshape(8, HD), q, k, v)


def solution(mesh):
    placed = (
        P(None, "ctx", "panel"),
        P(None, None, "panel"),
        P(None, "panel"),
        P(None, "ctx", "panel"),
        P(None, None, "panel"),
        P(None, "panel"),
        P("panel"),
        P("ctx", "panel"),
        P("ctx", "panel"),
        P("ctx", "panel"),
    )
    return jax.shard_map(
        functools.partial(body, mesh.shape["ctx"], mesh.shape["panel"]),
        mesh=mesh,
        in_specs=placed,
        out_specs=(P("ctx", "panel"), P("ctx", "panel"), P("ctx", "panel")),
        check_vma=False,
    )
```

time: 83.9 us -> 53.7 us (0.64)
  Pallas kernels: 0 us -> 48.5 us
  waiting for transfers between devices: 31.3 us -> 0 us
  starting transfers between devices: 12.6 us -> 0 us
  matrix products: 11.7 us -> 0 us
  local copies, waits for them, and re-layouts: 12.9 us -> 3.52 us
  other arithmetic: 7.55 us -> 0 us
  blocking collectives: 6.27 us -> 0 us
    pallas_call x0 -> x1, Pallas kernels: none -> 48.5 us  [body(): pl.pallas_call(functools.partial(kernel, n_ctx, n_panel), out_shape=(out,...]
    ppermute x4 -> x0, waiting for transfers between devices: 31.3 us -> none  [from_behind(): lax.ppermute(value, axis, [(source, source + steps) for source in range(f...]
    ppermute x4 -> x0, starting transfers between devices: 12.6 us -> none  [from_behind(): lax.ppermute(value, axis, [(source, source + steps) for source in range(f...]
    conv_general_dilated x2 -> x0, matrix products: 7.63 us -> none  [long_conv(): lax.conv_general_dilated(signal, reversed_taps, (1,), 'VALID', dimension_...]
    psum x1 -> x0, blocking collectives: 6.27 us -> none  [body(): lax.psum((jnp.sum(se_mix * se_mix, axis=-1), jnp.sum(mr_mix * mr_mix, axi...]
    slice x4 -> x0, local copies, waits for them, and re-layouts: 4.13 us -> none  [the longest x1 2.28 us: body(): medium_projected_streams[:, token_rows - (FEATURIZER_TAPS + MEDIUM_TAPS -...]
    dot_general x2 -> x0, matrix products: 4.04 us -> none  [the longest x1 2.47 us: attend(): jnp.einsum('hqk,khd->qhd', probs, v3, preferred_element_type=jnp.float32)]
    add x4 -> x0, other arithmetic: 3.54 us -> none  [the longest x2 3.53 us: featurize(): total + short[:, j][:, None, :] * ext[:, taps - 1 - j:count - j, :].astyp...]
  transfers between devices with their start and end apart: 4 -> 0, of which waited for: 3 -> 0; matrix products, arithmetic and copies ran while one was open for 18% -> 0% of each run, Pallas kernels for 0% -> 0%
where the time goes in v1:
time: 53.7 us; the launch traced here: 52.6 us
  Pallas kernels  48.5 us (90%)
  local copies, waits for them, and re-layouts  3.52 us (7%)
  between operations  0.65 us (1%)
    pallas_call x1, Pallas kernels, body(): pl.pallas_call(functools.partial(kernel, n_ctx, n_panel), out_shape=(out,...  48.5 us
    unnamed x7, local copies, waits for them, and re-layouts  3.52 us

profile of v1, /device:TPU:7, one launch (start us, length us, event | category | flops | bytes accessed | tf_op | source)
XLA Modules:
  0.0 52.6 jit_solution(13157581261973761757)
XLA Ops:
  0.6 48.5 %mixer.1 = (bf16[144,1024]{1,0:T(8,128)(2,1)}, bf16[144,1024]{1,0:T(8,128)(2,1)}, bf16[144,1024]{1,0:T(8,128)(2,1)}) custom-call(bf16[3,144,1024]{2,1,0:T(8,128)(2,1)} %se_u.1, f32[3,3,1024]{2,1,0:T(4,128)} %se_w.1, f32[7,1024]{1,0:T(8,128)} %se_f.1, bf16[3,144,1024]{2,1,0:T(8,128)(2,1)} %mr_u.1, f32[3,3,1024]{2,1,0:T(4,128)} %mr_w.1, f32[128,1024]{1,0:T(8,128)} %mr_raw.1, ...), custom_call_target="tpu_custom_call" | custom-call | tf_op jit(solution)/shard_map/mixer/pallas_call | solution.py:406
  49.1 0.0 copy-start.1
  49.1 1.7 %copy.16 = bf16[144,1024]{1,0:T(8,128)(2,1)} copy(bf16[144,1024]{1,0:T(8,128)(2,1)} %get-tuple-element.6) | data formatting | bytes 589824
  50.9 0.0 copy-done.1
  50.9 0.0 copy-start
  50.9 0.7 %copy.17 = bf16[144,1024]{1,0:T(8,128)(2,1)} copy(bf16[144,1024]{1,0:T(8,128)(2,1)S(1)} %copy-done.1) | data formatting | bytes 589824
  51.6 0.4 copy-done
  51.9 0.7 %copy.18 = bf16[144,1024]{1,0:T(8,128)(2,1)} copy(bf16[144,1024]{1,0:T(8,128)(2,1)S(1)} %copy-done) | data formatting | bytes 589824
Async XLA Ops:
  49.1 1.8 %copy-start.1 = (bf16[144,1024]{1,0:T(8,128)(2,1)S(1)}, bf16[144,1024]{1,0:T(8,128)(2,1)}, u32[]{:S(2)}) copy-start(bf16[144,1024]{1,0:T(8,128)(2,1)} %get-tuple-element.7) | copy-start | bytes 884740
  50.9 1.1 %copy-start = (bf16[144,1024]{1,0:T(8,128)(2,1)S(1)}, bf16[144,1024]{1,0:T(8,128)(2,1)}, u32[]{:S(2)}) copy-start(bf16[144,1024]{1,0:T(8,128)(2,1)} %get-tuple-element.8) | copy-start | bytes 884740

commit v2 on v1

--- a/solution.py
+++ b/solution.py
@@ -14,6 +14,9 @@
 TAPS = 128
 LSE = 7
 HEADS = 8
+PAIRS = HEADS // 2
+QUARTERS = 4
+PART_P = TAPS * 8 // QUARTERS
 WIDTH = HEADS * HD
 F32 = jnp.float32
 BF16 = jnp.bfloat16
@@ -57,8 +60,7 @@
     ub, wb, fb, rawb, decb, qb, kcat, vcat,
     ut, wt, ft, taps, se_p, mr_p, se_mix, mr_mix, at_mix, bias, sq,
     rim_out, rim_in, p_out, p_in, st_out, st_in,
-    load_sem, rim_sem, p_sem, k_send, k_recv, v_send, v_recv,
-    st_send, st_recv,
+    load_sem, rim_sem, p_send, p_recv, k_send, k_recv, v_send, v_recv, st_send, st_recv,
 ):
     c = lax.axis_index("ctx")
     p = lax.axis_index("panel")
@@ -75,6 +77,11 @@
         loads.append(copy)
         return copy
 
+    l_kv = []
+    for h in range(HEADS):
+        lanes = pl.ds(h * HD, HD)
+        l_kv.append(load(k.at[:, lanes], kcat.at[h, pl.ds(T, T), :]))
+        l_kv.append(load(v.at[:, lanes], vcat.at[h, pl.ds(T, T), :]))
     l_mr = [load(mr_u.at[i], ub.at[3 + i]) for i in (1, 2)]
     l_mw = load(mr_w, wb.at[1])
     l_sw = load(se_w, wb.at[0])
@@ -85,8 +92,6 @@
     l_raw = load(mr_raw, rawb)
     l_dec = load(decay, decb)
     l_q = load(q, qb)
-    l_k = load(k, kcat.at[pl.ds(T, T), :])
-    l_v = load(v, vcat.at[pl.ds(T, T), :])
 
     barrier = pltpu.get_barrier_semaphore()
 
@@ -112,6 +117,42 @@
     for i in range(6):
         ut[i, pl.ds(0, 16), :] = zero_halo
 
+    def own(ref, pair):
+        return ref.at[pl.ds(pair * 2, 2), pl.ds(T, T), :]
+
+    def prior(ref, pair):
+        return ref.at[pl.ds(pair * 2, 2), pl.ds(0, T), :]
+
+    def remote(source, target, send, recv, device):
+        return pltpu.make_async_remote_copy(
+            source, target, send, recv, device_id=device, device_id_type=MESH
+        )
+
+    rim_copy = remote(rim_out, rim_in, rim_sem.at[0], rim_sem.at[1], dst)
+
+    def p_part(ref, part):
+        return ref.at[pl.ds(part * PART_P, PART_P), :]
+
+    def p_copy(part):
+        return remote(p_part(p_out, part), p_part(p_in, part), p_send.at[part], p_recv.at[part], dst)
+
+    def k_copy(pair):
+        target = prior(kcat, pair)
+        return remote(own(kcat, pair), target, k_send.at[pair], k_recv.at[pair], dst)
+
+    def v_copy(pair):
+        target = prior(vcat, pair)
+        return remote(own(vcat, pair), target, v_send.at[pair], v_recv.at[pair], dst)
+
+    for copy in l_kv:
+        copy.wait()
+    pl.semaphore_wait(barrier, (n_panel - 1) + has_dst.astype(jnp.int32))
+
+    @pl.when(has_dst)
+    def _():
+        k_copy(0).start()
+        v_copy(0).start()
+
     def products(block, out, shift, t, count):
         first = feature(ut.at[block * 3 + 1], wt, block * 9 + 3, t, count)
         second = feature(ut.at[block * 3 + 2], wt, block * 9 + 6, t, count)
@@ -141,6 +182,11 @@
         copy.wait()
     for i in (1, 2):
         to_time(ub.at[i], ut.at[i], 2)
+
+    @pl.when(has_dst)
+    def _():
+        for part in range(QUARTERS):
+            p_copy(part).start()
 
     def se_low(i, carry):
         products(0, se_p, 8, i * 8, 8)
@@ -155,41 +201,15 @@
     for i in range(6):
         rim_out[pl.ds(64 + i * 16, 16), :] = ut[i, pl.ds(T * 8, 16), :].astype(BF16)
 
-    pl.semaphore_wait(barrier, (n_panel - 1) + has_dst.astype(jnp.int32))
-
-    def head(h):
-        return pl.ds(pl.multiple_of(h * HD, HD), HD)
-
-    rim_copy = pltpu.make_async_remote_copy(
-        rim_out, rim_in, rim_sem.at[0], rim_sem.at[1], device_id=dst, device_id_type=MESH
-    )
-    p_copy = pltpu.make_async_remote_copy(
-        p_out, p_in, p_sem.at[0], p_sem.at[1], device_id=dst, device_id_type=MESH
-    )
-
-    def k_copy(h):
-        return pltpu.make_async_remote_copy(
-            k.at[:, head(h)], kcat.at[pl.ds(0, T), head(h)], k_send.at[h], k_recv.at[h],
-            device_id=dst, device_id_type=MESH,
-        )
-
-    def v_copy(h):
-        return pltpu.make_async_remote_copy(
-            v.at[:, head(h)], vcat.at[pl.ds(0, T), head(h)], v_send.at[h], v_recv.at[h],
-            device_id=dst, device_id_type=MESH,
-        )
-
     @pl.when(has_dst)
     def _():
         rim_copy.start()
-        p_copy.start()
-
-        def send(h, carry):
-            k_copy(h).start()
-            v_copy(h).start()
-            return carry
-
-        lax.fori_loop(0, HEADS, send, 0)
+        for pair in range(1, PAIRS):
+            k_copy(pair).start()
+            v_copy(pair).start()
+
+    def head(h):
+        return pl.ds(pl.multiple_of(h * HD, HD), HD)
 
     l_f.wait()
     for j in range(LSE):
@@ -207,12 +227,13 @@
 
     lax.fori_loop(0, TAPS // 8, tap_rows, 0)
 
-    def tap_decay(j, carry):
-        jf = j.astype(F32)
-        taps[rows(j, 1), :] = taps[rows(j, 1), :] * jnp.exp(-decb[...] * jf)
-        return carry
-
-    lax.fori_loop(0, TAPS, tap_decay, 0)
+    def tap_decay(g, carry):
+        for jj in range(8):
+            j = g * 8 + jj
+            taps[rows(j, 1), :] = taps[rows(j, 1), :] * jnp.exp(-decb[...] * j.astype(F32))
+        return carry
+
+    lax.fori_loop(0, TAPS // 8, tap_decay, 0)
 
     queries_at = lax.broadcasted_iota(jnp.int32, (T, 2 * T), 0)
     keys_at = lax.broadcasted_iota(jnp.int32, (T, 2 * T), 1)
@@ -227,15 +248,10 @@
     def _():
         rim_in[...] = jnp.zeros((160, HD), BF16)
         p_in[...] = jnp.zeros((TAPS * 8, HD), BF16)
-        kcat[pl.ds(0, T), :] = jnp.zeros((T, WIDTH), BF16)
-        vcat[pl.ds(0, T), :] = jnp.zeros((T, WIDTH), BF16)
-
-    when_fed(rim_copy.wait_recv)
-    for i in range(6):
-        ut[i, pl.ds(0, 16), :] = rim_in[pl.ds(64 + i * 16, 16), :].astype(F32)
-    se_p[pl.ds(0, 64), :] = rim_in[pl.ds(0, 64), :].astype(F32)
-    products(0, se_p, 8, 0, 2)
-    products(1, mr_p, TAPS, 0, 2)
+        for h in range(HEADS):
+            kcat[h, pl.ds(0, T), :] = jnp.zeros((T, HD), BF16)
+            vcat[h, pl.ds(0, T), :] = jnp.zeros((T, HD), BF16)
+
 
     def se_block(i, carry):
         t = i * 8
@@ -245,39 +261,35 @@
         se_mix[rows(t, 8), :] = total * feature(ut.at[0], wt, 0, t, 8)
         return carry
 
-    lax.fori_loop(0, T // 8, se_block, 0)
-
-    when_fed(p_copy.wait_recv)
-
-    def prev_p(i, carry):
-        mr_p[rows(i * 8, 8), :] = p_in[rows(i * 8, 8), :].astype(F32)
-        return carry
-
-    lax.fori_loop(0, TAPS // 8, prev_p, 0)
+    lax.fori_loop(1, T // 8, se_block, 0)
+
 
     block = 16
 
-    def mr_block(i, carry):
+    def tap_group(t, g, acc):
+        j0 = g * 8
+        acc = list(acc)
+        window = [mr_p[rows(TAPS + t - j0 - 7 + s, 1), :] for s in range(block + 7)]
+        for jj in range(8):
+            tap = taps[rows(j0 + jj, 1), :]
+            for s in range(block):
+                acc[s] = acc[s] + tap * window[s + 7 - jj]
+        return tuple(acc)
+
+    def mr_own(i, carry):
         t = i * block
-
-        def tap_group(g, acc):
-            j0 = g * 8
-            acc = list(acc)
-            window = [mr_p[rows(TAPS + t - j0 - 7 + s, 1), :] for s in range(block + 7)]
-            for jj in range(8):
-                tap = taps[rows(j0 + jj, 1), :]
-                for s in range(block):
-                    acc[s] = acc[s] + tap * window[s + 7 - jj]
-            return tuple(acc)
-
         zero = jnp.zeros((8, HD), F32)
-        acc = lax.fori_loop(0, TAPS // 8, tap_group, (zero,) * block)
-        gate = feature(ut.at[3], wt, 9, t, block)
+        acc = lax.fori_loop(0, i * 2 - 1, lambda g, acc: tap_group(t, g, acc), (zero,) * block)
         for s in range(block):
-            mr_mix[rows(t + s, 1), :] = acc[s] * gate[s * 8 : s * 8 + 8]
-        return carry
-
-    lax.fori_loop(0, T // block, mr_block, 0)
+            mr_mix[rows(t + s, 1), :] = acc[s]
+        return carry
+
+    for s in range(block):
+        mr_mix[rows(s, 1), :] = jnp.zeros((8, HD), F32)
+    lax.fori_loop(1, T // block, mr_own, 0)
+
+    l_q.wait()
+    sq[2] = jnp.zeros((T, HD), F32)
 
     def squares(mix, out_index):
         def step(i, carry):
@@ -321,38 +333,70 @@
             precision=HIGHEST, preferred_element_type=F32,
         )
 
+    def attend(h, carry):
+        scores = lax.dot_general(
+            qb[:, head(h)], kcat[h], (((1,), (1,)), ((), ())),
+            preferred_element_type=F32,
+        )
+        scores = scores * (1.0 / math.sqrt(HD)) + bias[...]
+        top = jnp.max(scores, axis=1, keepdims=True)
+        raw = jnp.exp(scores - top)
+        total = jnp.sum(raw, axis=1, keepdims=True)
+        mixed = lax.dot_general(
+            raw.astype(BF16), vcat[h], (((1,), (0,)), ((), ())),
+            preferred_element_type=F32,
+        )
+        mixed = mixed * (1.0 / total)
+        at_mix[:, head(h)] = mixed
+        sq[2] = sq[2] + mixed * mixed
+        return carry
+
+    def attend_pair(pair):
+        when_fed(k_copy(pair).wait_recv)
+        when_fed(v_copy(pair).wait_recv)
+        lax.fori_loop(pair * 2, pair * 2 + 2, attend, 0)
+
+    attend_pair(0)
+
+
+    when_fed(rim_copy.wait_recv)
+    for i in range(6):
+        ut[i, pl.ds(0, 16), :] = rim_in[pl.ds(64 + i * 16, 16), :].astype(F32)
+    se_p[pl.ds(0, 64), :] = rim_in[pl.ds(0, 64), :].astype(F32)
+    products(0, se_p, 8, 0, 2)
+    products(1, mr_p, TAPS, 0, 2)
+    se_block(0, 0)
+    for part in range(QUARTERS):
+        when_fed(p_copy(part).wait_recv)
+
+    def prev_p(i, carry):
+        mr_p[rows(i * 8, 8), :] = p_in[rows(i * 8, 8), :].astype(F32)
+        return carry
+
+    lax.fori_loop(0, TAPS // 8, prev_p, 0)
+
+    def mr_rest(i, carry):
+        t = i * block
+        acc = tuple(mr_mix[rows(t + s, 1), :] for s in range(block))
+        start = lax.max(i * 2 - 1, 0)
+        acc = lax.fori_loop(start, TAPS // 8, lambda g, acc: tap_group(t, g, acc), acc)
+        gate = feature(ut.at[3], wt, 9, t, block)
+        for s in range(block):
+            mr_mix[rows(t + s, 1), :] = acc[s] * gate[s * 8 : s * 8 + 8]
+
+        return carry
+
+    lax.fori_loop(0, T // block, mr_rest, 0)
+
+    attend_pair(1)
+
     squares(se_mix, 0)
     squares(mr_mix, 1)
     st_out[0, 0, :, :T] = row_sums(0)
     st_out[0, 1, :, :T] = row_sums(1)
     share(0)
 
-    l_q.wait()
-    l_k.wait()
-    l_v.wait()
-    sq[2] = jnp.zeros((T, HD), F32)
-
-    def attend(h, carry):
-        when_fed(k_copy(h).wait_recv)
-        scores = lax.dot_general(
-            qb[:, head(h)], kcat[:, head(h)], (((1,), (1,)), ((), ())),
-            preferred_element_type=F32,
-        )
-        scores = scores * (1.0 / math.sqrt(HD)) + bias[...]
-        top = jnp.max(scores, axis=1, keepdims=True)
-        raw = jnp.exp(scores - top)
-        total = jnp.sum(raw, axis=1, keepdims=True)
-        when_fed(v_copy(h).wait_recv)
-        mixed = lax.dot_general(
-            raw.astype(BF16), vcat[:, head(h)], (((1,), (0,)), ((), ())),
-            preferred_element_type=F32,
-        )
-        mixed = mixed * (1.0 / total)
-        at_mix[:, head(h)] = mixed
-        sq[2] = sq[2] + mixed * mixed
-        return carry
-
-    lax.fori_loop(0, HEADS - 2, attend, 0)
+    attend_pair(2)
 
     for r in range(1, n_panel):
         st_copy(0, r).wait_recv()
@@ -371,7 +415,7 @@
 
         lax.fori_loop(0, T // 16, finish, 0)
 
-    lax.fori_loop(HEADS - 2, HEADS, attend, 0)
+    attend_pair(3)
 
     st_out[1, 0, :, :T] = row_sums(2)
     share(1)
@@ -388,22 +432,30 @@
     @pl.when(has_dst)
     def _():
         rim_copy.wait_send()
-        p_copy.wait_send()
-
-        def sent(h, carry):
-            k_copy(h).wait_send()
-            v_copy(h).wait_send()
-            return carry
-
-        lax.fori_loop(0, HEADS, sent, 0)
+        for part in range(QUARTERS):
+            p_copy(part).wait_send()
+        for pair in range(PAIRS):
+            k_copy(pair).wait_send()
+            v_copy(pair).wait_send()
+
+
+def writer(a, b, c, x, y, z, sems):
+    copies = [
+        pltpu.make_async_copy(i, o, sems.at[n]) for n, (i, o) in enumerate(((a, x), (b, y), (c, z)))
+    ]
+    for copy in copies:
+        copy.start()
+    for copy in copies:
+        copy.wait()
 
 
 def body(n_ctx, n_panel, se_u, se_w, se_f, mr_u, mr_w, mr_raw, mr_decay, q, k, v):
     anywhere = pl.BlockSpec(memory_space=pl.ANY)
     vmem = pl.BlockSpec(memory_space=pltpu.VMEM)
-    out = jax.ShapeDtypeStruct((T, WIDTH), BF16)
+    out = pltpu.VMEM((T, WIDTH), BF16)
+    plain = jax.ShapeDtypeStruct((T, WIDTH), BF16)
     dma = pltpu.SemaphoreType.DMA
-    return pl.pallas_call(
+    mixed = pl.pallas_call(
         functools.partial(kernel, n_ctx, n_panel),
         out_shape=(out, out, out),
         in_specs=[anywhere] * 10,
@@ -415,8 +467,8 @@
             pltpu.VMEM((TAPS, WIDTH), F32),
             pltpu.VMEM((8, HD), F32),
             pltpu.VMEM((T, WIDTH), BF16),
-            pltpu.VMEM((2 * T, WIDTH), BF16),
-            pltpu.VMEM((2 * T, WIDTH), BF16),
+            pltpu.VMEM((HEADS, 2 * T, HD), BF16),
+            pltpu.VMEM((HEADS, 2 * T, HD), BF16),
             pltpu.VMEM((6, (T + 2) * 8, HD), F32),
             pltpu.VMEM((18 * 8, HD), F32),
             pltpu.VMEM((8 * 8, HD), F32),
@@ -434,19 +486,28 @@
             pltpu.VMEM((TAPS * 8, HD), BF16),
             pltpu.VMEM((2, 2, 8, 256), F32),
             pltpu.VMEM((2, n_panel - 1, 2, 8, 256), F32),
-            dma((14,)),
+            dma((12 + 2 * HEADS,)),
             dma((2,)),
-            dma((2,)),
-            dma((HEADS,)),
-            dma((HEADS,)),
-            dma((HEADS,)),
-            dma((HEADS,)),
+            dma((QUARTERS,)),
+            dma((QUARTERS,)),
+            dma((PAIRS,)),
+            dma((PAIRS,)),
+            dma((PAIRS,)),
+            dma((PAIRS,)),
             dma((2, n_panel - 1)),
             dma((2, n_panel - 1)),
         ],
         compiler_params=pltpu.CompilerParams(collective_id=0, has_side_effects=True),
         name="mixer",
     )(se_u, se_w, se_f, mr_u, mr_w, mr_raw, mr_decay.reshape(8, HD), q, k, v)
+    return pl.pallas_call(
+        writer,
+        out_shape=(plain, plain, plain),
+        in_specs=[vmem] * 3,
+        out_specs=[anywhere] * 3,
+        scratch_shapes=[dma((3,))],
+        name="writer",
+    )(*(pltpu.with_memory_space_constraint(x, pltpu.VMEM) for x in mixed))
 
 
 def solution(mesh):

time: 53.7 us -> 49.1 us (0.914); the launches traced: 52.6 us -> 48.9 us
  local copies, waits for them, and re-layouts: 3.52 us -> 0 us
    unnamed x7 -> x0, local copies, waits for them, and re-layouts: 3.52 us -> none
    pallas_call x1, Pallas kernels: 48.5 us -> 47.4 us  [body(): pl.pallas_call(functools.partial(kernel, n_ctx, n_panel), out_shape=(out,...]
    pallas_call x0 -> x1, Pallas kernels: none -> 0.94 us  [body(): pl.pallas_call(writer, out_shape=(plain, plain, plain), in_specs=[vmem] *...]
where the time goes in v2:
time: 49.1 us; the launch traced here: 48.9 us
  Pallas kernels  48.3 us (98%)
  between operations  0.64 us (1%)
    pallas_call x1, Pallas kernels, body(): pl.pallas_call(functools.partial(kernel, n_ctx, n_panel), out_shape=(out,...  47.4 us

profile of v2, /device:TPU:7, one launch (start us, length us, event | category | flops | bytes accessed | tf_op | source)
XLA Modules:
  0.0 48.9 jit_solution(5547407578003340832)
XLA Ops:
  0.6 47.4 %mixer.1 = (bf16[144,1024]{1,0:T(8,128)(2,1)S(1)}, bf16[144,1024]{1,0:T(8,128)(2,1)S(1)}, bf16[144,1024]{1,0:T(8,128)(2,1)S(1)}) custom-call(bf16[3,144,1024]{2,1,0:T(8,128)(2,1)} %se_u.1, f32[3,3,1024]{2,1,0:T(4,128)} %se_w.1, f32[7,1024]{1,0:T(8,128)} %se_f.1, bf16[3,144,1024]{2,1,0:T(8,128)(2,1)} %mr_u.1, f32[3,3,1024]{2,1,0:T(4,128)} %mr_w.1, ...), custom_call_target="tpu_custom_call" | custom-call | tf_op jit(solution)/shard_map/mixer/pallas_call | solution.py:458
  48.0 0.9 %writer.1 = (bf16[144,1024]{1,0:T(8,128)(2,1)}, bf16[144,1024]{1,0:T(8,128)(2,1)}, bf16[144,1024]{1,0:T(8,128)(2,1)}) custom-call(bf16[144,1024]{1,0:T(8,128)(2,1)S(1)} %get-tuple-element.6.a, bf16[144,1024]{1,0:T(8,128)(2,1)S(1)} %get-tuple-element.7.b, bf16[144,1024]{1,0:T(8,128)(2,1)S(1)} %get-tuple-element.8.c), custom_call_target="tpu_custom_call" | custom-call | tf_op jit(solution)/shard_map/writer/pallas_call | solution.py:503

commit v3 on v2

--- a/solution.py
+++ b/solution.py
@@ -104,6 +104,42 @@
             barrier, inc=1, device_id=(c, lax.rem(p + r, n_panel)), device_id_type=MESH
         )
 
+    def own(ref, pair):
+        return ref.at[pl.ds(pair * 2, 2), pl.ds(T, T), :]
+
+    def prior(ref, pair):
+        return ref.at[pl.ds(pair * 2, 2), pl.ds(0, T), :]
+
+    def remote(source, target, send, recv, device):
+        return pltpu.make_async_remote_copy(
+            source, target, send, recv, device_id=device, device_id_type=MESH
+        )
+
+    rim_copy = remote(rim_out, rim_in, rim_sem.at[0], rim_sem.at[1], dst)
+
+    def p_part(ref, part):
+        return ref.at[pl.ds(part * PART_P, PART_P), :]
+
+    def p_copy(part):
+        return remote(p_part(p_out, part), p_part(p_in, part), p_send.at[part], p_recv.at[part], dst)
+
+    def k_copy(pair):
+        target = prior(kcat, pair)
+        return remote(own(kcat, pair), target, k_send.at[pair], k_recv.at[pair], dst)
+
+    def v_copy(pair):
+        target = prior(vcat, pair)
+        return remote(own(vcat, pair), target, v_send.at[pair], v_recv.at[pair], dst)
+
+    for copy in l_kv[:4]:
+        copy.wait()
+    pl.semaphore_wait(barrier, (n_panel - 1) + has_dst.astype(jnp.int32))
+
+    @pl.when(has_dst)
+    def _():
+        k_copy(0).start()
+        v_copy(0).start()
+
     l_mw.wait()
     l_sw.wait()
     for b in range(2):
@@ -117,42 +153,6 @@
     for i in range(6):
         ut[i, pl.ds(0, 16), :] = zero_halo
 
-    def own(ref, pair):
-        return ref.at[pl.ds(pair * 2, 2), pl.ds(T, T), :]
-
-    def prior(ref, pair):
-        return ref.at[pl.ds(pair * 2, 2), pl.ds(0, T), :]
-
-    def remote(source, target, send, recv, device):
-        return pltpu.make_async_remote_copy(
-            source, target, send, recv, device_id=device, device_id_type=MESH
-        )
-
-    rim_copy = remote(rim_out, rim_in, rim_sem.at[0], rim_sem.at[1], dst)
-
-    def p_part(ref, part):
-        return ref.at[pl.ds(part * PART_P, PART_P), :]
-
-    def p_copy(part):
-        return remote(p_part(p_out, part), p_part(p_in, part), p_send.at[part], p_recv.at[part], dst)
-
-    def k_copy(pair):
-        target = prior(kcat, pair)
-        return remote(own(kcat, pair), target, k_send.at[pair], k_recv.at[pair], dst)
-
-    def v_copy(pair):
-        target = prior(vcat, pair)
-        return remote(own(vcat, pair), target, v_send.at[pair], v_recv.at[pair], dst)
-
-    for copy in l_kv:
-        copy.wait()
-    pl.semaphore_wait(barrier, (n_panel - 1) + has_dst.astype(jnp.int32))
-
-    @pl.when(has_dst)
-    def _():
-        k_copy(0).start()
-        v_copy(0).start()
-
     def products(block, out, shift, t, count):
         first = feature(ut.at[block * 3 + 1], wt, block * 9 + 3, t, count)
         second = feature(ut.at[block * 3 + 2], wt, block * 9 + 6, t, count)
@@ -160,7 +160,7 @@
         out[rows(t + shift, count), :] = rounded.astype(F32)
         return rounded
 
-    for copy in l_mr:
+    for copy in l_kv[4:] + l_mr:
         copy.wait()
     for i in (4, 5):
         to_time(ub.at[i], ut.at[i], 2)
@@ -207,9 +207,6 @@
         for pair in range(1, PAIRS):
             k_copy(pair).start()
             v_copy(pair).start()
-
-    def head(h):
-        return pl.ds(pl.multiple_of(h * HD, HD), HD)
 
     l_f.wait()
     for j in range(LSE):
@@ -333,28 +330,30 @@
             precision=HIGHEST, preferred_element_type=F32,
         )
 
-    def attend(h, carry):
+    def weigh(h):
+        lanes = slice(h * HD, (h + 1) * HD)
         scores = lax.dot_general(
-            qb[:, head(h)], kcat[h], (((1,), (1,)), ((), ())),
-            preferred_element_type=F32,
+            qb[:, lanes], kcat[h], (((1,), (1,)), ((), ())), preferred_element_type=F32
         )
         scores = scores * (1.0 / math.sqrt(HD)) + bias[...]
         top = jnp.max(scores, axis=1, keepdims=True)
         raw = jnp.exp(scores - top)
-        total = jnp.sum(raw, axis=1, keepdims=True)
+        return raw.astype(BF16), jnp.sum(raw, axis=1, keepdims=True)
+
+    def blend(h, raw, total):
+        lanes = slice(h * HD, (h + 1) * HD)
         mixed = lax.dot_general(
-            raw.astype(BF16), vcat[h], (((1,), (0,)), ((), ())),
-            preferred_element_type=F32,
+            raw, vcat[h], (((1,), (0,)), ((), ())), preferred_element_type=F32
         )
         mixed = mixed * (1.0 / total)
-        at_mix[:, head(h)] = mixed
-        sq[2] = sq[2] + mixed * mixed
-        return carry
+        at_mix[:, lanes] = mixed
+        return mixed * mixed
 
     def attend_pair(pair):
         when_fed(k_copy(pair).wait_recv)
+        one, two = weigh(pair * 2), weigh(pair * 2 + 1)
         when_fed(v_copy(pair).wait_recv)
-        lax.fori_loop(pair * 2, pair * 2 + 2, attend, 0)
+        sq[2] = sq[2] + (blend(pair * 2, *one) + blend(pair * 2 + 1, *two))
 
     attend_pair(0)
 

time: 49.1 us -> 48.1 us (0.980)
  Pallas kernels: 48.3 us -> 47.3 us
    pallas_call x1, Pallas kernels: 47.4 us -> 46.3 us  [body(): pl.pallas_call(functools.partial(kernel, n_ctx, n_panel), out_shape=(out,...]
where the time goes in v3:
time: 48.1 us; the launch traced here: 47.9 us
  Pallas kernels  47.3 us (98%)
  between operations  0.64 us (1%)
    pallas_call x1, Pallas kernels, body(): pl.pallas_call(functools.partial(kernel, n_ctx, n_panel), out_shape=(out,...  46.3 us

profile of v3, /device:TPU:7, one launch (start us, length us, event | category | flops | bytes accessed | tf_op | source)
XLA Modules:
  0.0 47.9 jit_solution(12443115496889053249)
XLA Ops:
  0.6 46.3 %mixer.1 = (bf16[144,1024]{1,0:T(8,128)(2,1)S(1)}, bf16[144,1024]{1,0:T(8,128)(2,1)S(1)}, bf16[144,1024]{1,0:T(8,128)(2,1)S(1)}) custom-call(bf16[3,144,1024]{2,1,0:T(8,128)(2,1)} %se_u.1, f32[3,3,1024]{2,1,0:T(4,128)} %se_w.1, f32[7,1024]{1,0:T(8,128)} %se_f.1, bf16[3,144,1024]{2,1,0:T(8,128)(2,1)} %mr_u.1, f32[3,3,1024]{2,1,0:T(4,128)} %mr_w.1, ...), custom_call_target="tpu_custom_call" | custom-call | tf_op jit(solution)/shard_map/mixer/pallas_call | solution.py:457
  47.0 0.9 %writer.1 = (bf16[144,1024]{1,0:T(8,128)(2,1)}, bf16[144,1024]{1,0:T(8,128)(2,1)}, bf16[144,1024]{1,0:T(8,128)(2,1)}) custom-call(bf16[144,1024]{1,0:T(8,128)(2,1)S(1)} %get-tuple-element.6.a, bf16[144,1024]{1,0:T(8,128)(2,1)S(1)} %get-tuple-element.7.b, bf16[144,1024]{1,0:T(8,128)(2,1)S(1)} %get-tuple-element.8.c), custom_call_target="tpu_custom_call" | custom-call | tf_op jit(solution)/shard_map/writer/pallas_call | solution.py:502
